TPU v7x, 512 devices: a whole 4x8x8 slice. The times are simulated.
512 devices in a mesh: dp: 64 (over y, x, core), tensor: 8 (over z).
Axes of the slice: x: 4, y: 8, z: 8, core: 2. Of those that a mesh axis runs over, the one named last changes fastest.
Arguments:
- hidden_act: bfloat16 [32768, 1408], P('dp', 'tensor'), may hold values from -6 to 6
- cotangent: bfloat16 [32768, 2048], P('dp', 'tensor'), may hold values from -4 to 4
- down_table: bfloat16 [1408, 64, 2048], P('tensor', 'dp'), may hold values from -0.15625 to 0.15625
- expert_ids: int32 [128, 4], P('dp'), may hold values from 0 to 31, as said below
- merge_weights: float32 [128, 4], P('dp'), may hold values from 0.1 to 1
- owner_slot: int32 [32], replicated, may hold values from 0 to 63, as said below
Outputs:
- layer_out: bfloat16 [32768, 2048], P('dp', 'tensor')
- grad_hidden: bfloat16 [32768, 1408], P('dp', 'tensor')
- expert_grad: float32 [1408, 64, 2048], P('tensor', 'dp')
Inputs may be any that keep to these rules, and one draw needn't show every extreme that they name: `expert_ids`: each segment lists 4 different experts; the 2 segments of one index of dp list exactly 6 different experts together. `owner_slot`: different experts have different slots; slot 63 always holds an expert.
All inputs are finite; a program needn't handle non-finite values.
Results may differ from a plain program's by a relative error of at most 0.013.
Values may be sent and summed in bfloat16 or wider, within the bound.
A program may use at most 128 MiB of HBM per device.

v0:
```python
import jax
import jax.numpy as jnp
from jax import lax
from jax.sharding import PartitionSpec as P

E = 32
K = 4
ROW_PARTS = 4
PAD = 4


def two_pieces(values):
    high = lax.reduce_precision(values, 8, 7)
    low = lax.reduce_precision(values - high, 8, 7)
    return (high, low)


def exchange(blocks):
    return lax.all_to_all(blocks, "dp", split_axis=0, concat_axis=0, tiled=True)


def split_panels(panels, count):
    lead, ff_local, width = panels.shape
    cols = count // ROW_PARTS
    view = panels.reshape(lead, ROW_PARTS, ff_local // ROW_PARTS, cols, width // cols)
    return jnp.transpose(view, (1, 3, 0, 2, 4)).reshape(
        count, lead, ff_local // ROW_PARTS, width // cols
    )


def join_panels(chunks):
    count, lead, rows, lanes = chunks.shape
    cols = count // ROW_PARTS
    view = chunks.reshape(ROW_PARTS, cols, lead, rows, lanes)
    return jnp.transpose(view, (2, 0, 3, 1, 4)).reshape(lead, ROW_PARTS * rows, cols * lanes)


def body(hidden_act, cotangent, down_table, expert_ids, merge_weights, owner_slot):
    count = lax.axis_size("dp")
    seg_count = expert_ids.shape[0]
    ff_local, _, width = down_table.shape
    row_count = hidden_act.shape[0]
    seg_len = row_count // seg_count
    rows = ff_local // ROW_PARTS
    lanes = width * ROW_PARTS // count
    listed = seg_count * K
    full_cot = lax.all_gather(cotangent, "tensor", axis=1, tiled=True)
    high, low = two_pieces(merge_weights)
    meta = jnp.concatenate(
        [expert_ids.astype(jnp.float32).reshape(-1), high.reshape(-1), low.reshape(-1)]
    ).astype(jnp.bfloat16)
    meta = jnp.pad(meta[None, :], ((0, PAD - 1), (0, lanes - 3 * listed)))
    table_chunks = split_panels(jnp.transpose(down_table, (1, 0, 2)), count)[:, 0]
    outgoing = jnp.concatenate(
        [table_chunks, jnp.broadcast_to(meta[None], (count, PAD, lanes))], axis=1
    )
    arrived = exchange(outgoing)
    by_slot = arrived[:, :rows]
    meta_all = arrived[:, rows, : 3 * listed].astype(jnp.float32)
    ids_all = meta_all[:, :listed].astype(jnp.int32).reshape(count * seg_count, K)
    high_all = meta_all[:, listed : 2 * listed].reshape(count * seg_count, K)
    low_all = meta_all[:, 2 * listed :].reshape(count * seg_count, K)
    experts = jnp.arange(E, dtype=jnp.int32)
    slots_all = jnp.sum(
        jnp.where(ids_all[:, :, None] == experts, owner_slot[None, None, :], 0), axis=2
    )
    hits = slots_all[:, :, None] == jnp.arange(count, dtype=jnp.int32)
    coef = jnp.concatenate(
        [
            jnp.sum(jnp.where(hits, high_all[:, :, None], 0.0), axis=1),
            jnp.sum(jnp.where(hits, low_all[:, :, None], 0.0), axis=1),
        ],
        axis=0,
    ).astype(jnp.bfloat16)
    halves = jnp.einsum("ms,srl->mrl", coef, by_slot, preferred_element_type=jnp.float32)
    merged_chunks = (halves[: count * seg_count] + halves[count * seg_count :]).astype(jnp.bfloat16)
    merged = join_panels(exchange(merged_chunks.reshape(count, seg_count, rows, lanes)))
    hidden_seg = hidden_act.reshape(seg_count, seg_len, ff_local)
    cot_seg = full_cot.reshape(seg_count, seg_len, width)
    seg_grads = jnp.einsum(
        "stf,std->sfd", hidden_seg, cot_seg, preferred_element_type=jnp.float32
    ).astype(jnp.bfloat16)
    returned = exchange(split_panels(seg_grads, count)).reshape(count * seg_count, rows, lanes)
    partial_rows = jnp.einsum(
        "stf,sfd->std", hidden_seg, merged, preferred_element_type=jnp.float32
    ).reshape(row_count, width)
    layer_out = lax.psum_scatter(
        partial_rows.astype(jnp.bfloat16), "tensor", scatter_dimension=1, tiled=True
    )
    grad_hidden = (
        jnp.einsum("std,sfd->stf", cot_seg, merged, preferred_element_type=jnp.float32)
        .astype(jnp.bfloat16)
        .reshape(row_count, ff_local)
    )
    by_segment = jnp.stack([coef[: count * seg_count], coef[count * seg_count :]], axis=1)
    slot_halves = jnp.einsum(
        "mhs,mrl->hsrl", by_segment, returned, preferred_element_type=jnp.float32
    )
    slot_grads = (slot_halves[0] + slot_halves[1]).astype(jnp.bfloat16)
    own_grad = join_panels(exchange(slot_grads)[:, None])
    expert_grad = jnp.transpose(own_grad, (1, 0, 2)).astype(jnp.float32)
    return (layer_out, grad_hidden, expert_grad)


def solution(mesh):
    placed = (
        P("dp", "tensor"),
        P("dp", "tensor"),
        P("tensor", "dp", None),
        P("dp", None),
        P("dp", None),
        P(),
    )
    return jax.shard_map(
        body,
        mesh=mesh,
        in_specs=placed,
        out_specs=(P("dp", "tensor"), P("dp", "tensor"), P("tensor", "dp", None)),
        check_vma=False,
    )
```

profile of v0, /device:TPU:1, one launch (start us, length us, event | category | flops | bytes accessed | tf_op | source)
XLA Modules:
  0.0 178.1 jit_solution(396525168196531516)
XLA Ops:
  8.8 1.3 copy.65
  10.4 1.0 pad_maximum_fusion
  11.4 11.8 %all-to-all-start = ((bf16[64,48,128]{2,1,0:T(8,128)(2,1)}), bf16[64,48,128]{2,1,0:T(8,128)(2,1)S(1)}, u32[]{:S(2)}, u32[]{:S(2)}) async-start(bf16[64,48,128]{2,1,0:T(8,128)(2,1)} %pad_maximum_fusion), calls=%async_computation | async-start | bytes 1572864 | tf_op jit(solution)/shard_map/all_to_all | solution.py:19
  23.9 22.0 %all-to-all-done = bf16[64,48,128]{2,1,0:T(8,128)(2,1)S(1)} async-done(((bf16[64,48,128]{2,1,0:T(8,128)(2,1)}), bf16[64,48,128]{2,1,0:T(8,128)(2,1)S(1)}, u32[]{:S(2)}, u32[]{:S(2)}) %all-to-all-start) | async-done | bytes 786464 | tf_op jit(solution)/shard_map/all_to_all | solution.py:19
  46.6 0.9 fusion.4
  48.1 2.1 %copy.51 = bf16[64,2,44,128]{3,1,2,0:T(2,128)(2,1)} copy(bf16[64,2,44,128]{3,1,0,2:T(2,128)(2,1)S(1)} %bitcast.66) | data formatting | bytes 2883584 | tf_op jit(solution)/shard_map/reshape | solution.py:77
  50.2 6.4 %all-to-all-start.1 = ((bf16[64,2,44,128]{3,1,2,0:T(2,128)(2,1)}), bf16[64,2,44,128]{3,1,2,0:T(2,128)(2,1)S(1)}, u32[]{:S(2)}, u32[]{:S(2)}) async-start(bf16[64,2,44,128]{3,1,2,0:T(2,128)(2,1)} %copy.51), calls=%async_computation.1 | async-start | bytes 2883584 | tf_op jit(solution)/shard_map/all_to_all | solution.py:19
  56.6 20.5 %all-gather.2.cloned.1.call-done = bf16[512,2048]{1,0:T(8,128)(2,1)} async-done(((bf16[512,256]{1,0:T(8,128)(2,1)}), bf16[512,2048]{1,0:T(8,128)(2,1)}) %all-gather.2.cloned.1.call-update) | async-done | bytes 2097168 | tf_op jit(solution)/shard_map/all_gather | solution.py:47
  77.1 2.1 %convolution_convert_fusion.1 = bf16[2,176,2048]{2,1,0:T(8,128)(2,1)S(1)} fusion(bf16[2,256,2048]{2,1,0:T(8,128)(2,1)} %bitcast.63, bf16[22,2,8,256]{3,2,1,0:T(8,128)(2,1)S(1)} %bitcast.77), kind=kOutput, calls=%fused_computation.3 | convolution fusion | flops 369819648 | bytes 3719168 | tf_op jit(solution)/shard_map/stf,std->sfd/dot_general | solution.py:80
  80.0 2.6 %copy.57 = bf16[64,2,44,128]{3,1,2,0:T(2,128)(2,1)} copy(bf16[64,2,44,128]{3,0,2,1:T(8,128)(2,1)S(1)} %bitcast.71) | data formatting | bytes 2883584 | tf_op jit(solution)/shard_map/reshape | solution.py:26
  82.6 10.3 %all-to-all-done.1 = bf16[64,2,44,128]{3,1,2,0:T(2,128)(2,1)S(1)} async-done(((bf16[64,2,44,128]{3,1,2,0:T(2,128)(2,1)}), bf16[64,2,44,128]{3,1,2,0:T(2,128)(2,1)S(1)}, u32[]{:S(2)}, u32[]{:S(2)}) %all-to-all-start.1) | async-done | bytes 1441824 | tf_op jit(solution)/shard_map/all_to_all | solution.py:19
  92.9 6.3 %all-to-all-start.2 = ((bf16[64,2,44,128]{3,1,2,0:T(2,128)(2,1)}), bf16[64,2,44,128]{3,1,2,0:T(2,128)(2,1)S(1)}, u32[]{:S(2)}, u32[]{:S(2)}) async-start(bf16[64,2,44,128]{3,1,2,0:T(2,128)(2,1)} %copy.57), calls=%async_computation.3 | async-start | bytes 2883584 | tf_op jit(solution)/shard_map/all_to_all | solution.py:19
  99.4 1.3 copy.78
  100.7 2.5 %reshape.114 = bf16[2,176,2048]{2,1,0:T(8,128)(2,1)S(1)} reshape(bf16[2,4,44,16,128]{4,3,2,1,0:T(8,128)(2,1)} %bitcast.72) | data formatting | bytes 2883584 | tf_op jit(solution)/shard_map/reshape | solution.py:35
  103.2 2.1 %convolution_convert_fusion = bf16[2,2048,256]{1,2,0:T(8,128)(2,1)} fusion(bf16[2,176,2048]{2,1,0:T(8,128)(2,1)S(1)} %reshape.114, bf16[22,2,8,256]{3,2,1,0:T(8,128)(2,1)S(1)} %bitcast.78), kind=kOutput, calls=%fused_computation | convolution fusion | flops 370147328 | bytes 3719168 | tf_op jit(solution)/shard_map/stf,sfd->std/dot_general | solution.py:84
  105.3 30.3 %all-to-all-done.2 = bf16[64,2,44,128]{3,1,2,0:T(2,128)(2,1)S(1)} async-done(((bf16[64,2,44,128]{3,1,2,0:T(2,128)(2,1)}), bf16[64,2,44,128]{3,1,2,0:T(2,128)(2,1)S(1)}, u32[]{:S(2)}, u32[]{:S(2)}) %all-to-all-start.2) | async-done | bytes 1441824 | tf_op jit(solution)/shard_map/all_to_all | solution.py:19
  135.6 1.5 copy.58
  137.9 1.4 copy.59
  139.3 6.5 %all-to-all-start.3 = ((bf16[64,44,128]{2,1,0:T(8,128)(2,1)}), bf16[64,44,128]{2,1,0:T(8,128)(2,1)}, u32[]{:S(2)}, u32[]{:S(2)}) async-start(bf16[64,44,128]{2,1,0:T(8,128)(2,1)} %copy.59), calls=%async_computation.4 | async-start | bytes 1572864 | tf_op jit(solution)/shard_map/all_to_all | solution.py:19
  145.8 0.8 fusion.2
  146.6 0.7 copy.64
  147.3 21.1 %all-to-all-done.3 = bf16[64,44,128]{2,1,0:T(8,128)(2,1)} async-done(((bf16[64,44,128]{2,1,0:T(8,128)(2,1)}), bf16[64,44,128]{2,1,0:T(8,128)(2,1)}, u32[]{:S(2)}, u32[]{:S(2)}) %all-to-all-start.3) | async-done | bytes 720928 | tf_op jit(solution)/shard_map/all_to_all | solution.py:19
  168.5 1.3 convert_bitcast_fusion
  169.7 1.5 copy.60
  (34 shorter events, 5.7 us)
Async XLA Ops:
  11.4 35.1 %copy-start.2 = (s32[32]{0:T(128)S(1)}, s32[32]{0:T(128)}, u32[]{:S(2)}) copy-start(s32[32]{0:T(128)} %param.11) | copy-start | bytes 388
  11.4 34.5 %all-to-all-start = ((bf16[64,48,128]{2,1,0:T(8,128)(2,1)}), bf16[64,48,128]{2,1,0:T(8,128)(2,1)S(1)}, u32[]{:S(2)}, u32[]{:S(2)}) async-start(bf16[64,48,128]{2,1,0:T(8,128)(2,1)} %pad_maximum_fusion), calls=%async_computation | async-start | bytes 1572864 | tf_op jit(solution)/shard_map/all_to_all | solution.py:19
  23.1 54.0 %all-gather.2.cloned.1.call-start = ((), (), s32[]{:S(2)}) async-start(), calls=%async_computation.6 | async-start | bytes 2359296 | tf_op jit(solution)/shard_map/all_gather | solution.py:47
  50.2 26.9 %copy-start.1 = (bf16[512,176]{0,1:T(8,128)(2,1)S(1)}, bf16[512,176]{0,1:T(8,128)(2,1)}, u32[]{:S(2)}) copy-start(bf16[512,176]{0,1:T(8,128)(2,1)} %param.6) | copy-start | bytes 540676
  50.2 42.7 %all-to-all-start.1 = ((bf16[64,2,44,128]{3,1,2,0:T(2,128)(2,1)}), bf16[64,2,44,128]{3,1,2,0:T(2,128)(2,1)S(1)}, u32[]{:S(2)}, u32[]{:S(2)}) async-start(bf16[64,2,44,128]{3,1,2,0:T(2,128)(2,1)} %copy.51), calls=%async_computation.1 | async-start | bytes 2883584 | tf_op jit(solution)/shard_map/all_to_all | solution.py:19
  92.9 42.7 %all-to-all-start.2 = ((bf16[64,2,44,128]{3,1,2,0:T(2,128)(2,1)}), bf16[64,2,44,128]{3,1,2,0:T(2,128)(2,1)S(1)}, u32[]{:S(2)}, u32[]{:S(2)}) async-start(bf16[64,2,44,128]{3,1,2,0:T(2,128)(2,1)} %copy.57), calls=%async_computation.3 | async-start | bytes 2883584 | tf_op jit(solution)/shard_map/all_to_all | solution.py:19
  99.2 72.1 %reduce-scatter.2.cloned.1.call-start = ((), (), s32[]{:S(2)}) async-start(), calls=%async_computation.5 | async-start | bytes 2359296 | tf_op jit(solution)/shard_map/reduce_scatter | solution.py:87
  137.9 7.8 %copy-start = (bf16[512,2048]{1,0:T(8,128)(2,1)S(1)}, bf16[512,2048]{1,0:T(8,128)(2,1)}, u32[]{:S(2)}) copy-start(bf16[512,2048]{1,0:T(8,128)(2,1)} %all-gather.2.cloned.1.call-done) | copy-start | bytes 6291460
  139.3 29.2 %all-to-all-start.3 = ((bf16[64,44,128]{2,1,0:T(8,128)(2,1)}), bf16[64,44,128]{2,1,0:T(8,128)(2,1)}, u32[]{:S(2)}, u32[]{:S(2)}) async-start(bf16[64,44,128]{2,1,0:T(8,128)(2,1)} %copy.59), calls=%async_computation.4 | async-start | bytes 1572864 | tf_op jit(solution)/shard_map/all_to_all | solution.py:19
Sparse Core Ops, SparseCore 0:
  26.0 51.0 all-gather.1
  105.4 45.6 reduce-scatter.1
where the time goes:
time: 179 us; the launch traced here: 178 us
  waiting for transfers between devices  105 us (59%)
  starting transfers between devices  31.1 us (17%)
  local copies, waits for them, and re-layouts  16.5 us (9%)
  between operations  14.2 us (8%)
  matrix products  6.5 us (4%)
  other arithmetic  4.78 us (3%)
    all_to_all x4, waiting for transfers between devices, exchange(): return lax.all_to_all(blocks, 'dp', split_axis=0, concat_axis=0, tiled=True)  83.7 us
    all_to_all x4, starting transfers between devices, exchange(): return lax.all_to_all(blocks, 'dp', split_axis=0, concat_axis=0, tiled=True)  30.9 us
    all_gather x1, waiting for transfers between devices, body(): full_cot = lax.all_gather(cotangent, 'tensor', axis=1, tiled=True)  20.5 us
  transfers between devices with their start and end apart: 6, of which 5 were waited for; matrix products, arithmetic and copies ran while one was open for 13% of the time, Pallas kernels for 0%

commit v1 on v0

--- a/solution.py
+++ b/solution.py
@@ -7,6 +7,11 @@
 K = 4
 ROW_PARTS = 4
 PAD = 4
+
+
+def all_by_exchange(x, mesh_axis, along):
+    sent = jnp.stack([x] * lax.axis_size(mesh_axis))
+    return jnp.concatenate(lax.all_to_all(sent, mesh_axis, 0, 0), axis=along)
 
 
 def two_pieces(values):
@@ -44,7 +49,7 @@
     rows = ff_local // ROW_PARTS
     lanes = width * ROW_PARTS // count
     listed = seg_count * K
-    full_cot = lax.all_gather(cotangent, "tensor", axis=1, tiled=True)
+    full_cot = all_by_exchange(cotangent, "tensor", 1)
     high, low = two_pieces(merge_weights)
     meta = jnp.concatenate(
         [expert_ids.astype(jnp.float32).reshape(-1), high.reshape(-1), low.reshape(-1)]

time: 179 us -> 238 us (1.33)
  blocking collectives: 0 us -> 34.2 us
  waiting for transfers between devices: 105 us -> 121 us
  local copies, waits for them, and re-layouts: 16.5 us -> 24.8 us
    all_to_all x0 -> x1, waiting for transfers between devices: none -> 44.1 us  [all_by_exchange(): return jnp.concatenate(lax.all_to_all(sent, mesh_axis, 0, 0), axis=along)]
    all_to_all x0 -> x1, blocking collectives: none -> 34.2 us  [exchange(): return lax.all_to_all(blocks, 'dp', split_axis=0, concat_axis=0, tiled=True)]
    all_gather x1 -> x0, waiting for transfers between devices: 20.5 us -> none  [body(): full_cot = lax.all_gather(cotangent, 'tensor', axis=1, tiled=True)]
    all_to_all x0 -> x1, starting transfers between devices: none -> 10.2 us  [all_by_exchange(): return jnp.concatenate(lax.all_to_all(sent, mesh_axis, 0, 0), axis=along)]
    all_to_all x4 -> x3, starting transfers between devices: 30.9 us -> 22 us  [exchange(): return lax.all_to_all(blocks, 'dp', split_axis=0, concat_axis=0, tiled=True)]
    all_to_all x4 -> x3, waiting for transfers between devices: 83.7 us -> 76.5 us  [exchange(): return lax.all_to_all(blocks, 'dp', split_axis=0, concat_axis=0, tiled=True)]
    another operation x0 -> x2, local copies, waits for them, and re-layouts: none -> 4.36 us  [the longest x1 2.87 us: body(): cot_seg = full_cot.reshape(seg_count, seg_len, width)]
    reshape x0 -> x1, local copies, waits for them, and re-layouts: none -> 2.53 us  [all_by_exchange(): return jnp.concatenate(lax.all_to_all(sent, mesh_axis, 0, 0), axis=along)]
  transfers between devices with their start and end apart: 6 -> 5, of which waited for: 5 -> 4; matrix products, arithmetic and copies ran while one was open for 13% -> 13% of each run, Pallas kernels for 0% -> 0%
where the time goes in v1:
time: 238 us; the launch traced here: 237 us
  waiting for transfers between devices  121 us (51%)
  blocking collectives  34.2 us (14%)
  starting transfers between devices  32.4 us (14%)
  local copies, waits for them, and re-layouts  24.8 us (10%)
  between operations  14.2 us (6%)
  matrix products  6.81 us (3%)
  other arithmetic  3.9 us (2%)
    all_to_all x3, waiting for transfers between devices, exchange(): return lax.all_to_all(blocks, 'dp', split_axis=0, concat_axis=0, tiled=True)  76.5 us
    all_to_all x1, waiting for transfers between devices, all_by_exchange(): return jnp.concatenate(lax.all_to_all(sent, mesh_axis, 0, 0), axis=along)  44.1 us
    all_to_all x1, blocking collectives, exchange(): return lax.all_to_all(blocks, 'dp', split_axis=0, concat_axis=0, tiled=True)  34.2 us
    all_to_all x3, starting transfers between devices, exchange(): return lax.all_to_all(blocks, 'dp', split_axis=0, concat_axis=0, tiled=True)  22 us
    all_to_all x1, starting transfers between devices, all_by_exchange(): return jnp.concatenate(lax.all_to_all(sent, mesh_axis, 0, 0), axis=along)  10.2 us
  transfers between devices with their start and end apart: 5, of which 4 were waited for; matrix products, arithmetic and copies ran while one was open for 13% of the time, Pallas kernels for 0%

profile of v1, /device:TPU:1, one launch (start us, length us, event | category | flops | bytes accessed | tf_op | source)
XLA Modules:
  0.0 236.9 jit_solution(8688452059037920195)
XLA Ops:
  8.8 1.3 copy.68
  10.5 34.2 %all_to_all.25 = bf16[64,48,128]{2,1,0:T(8,128)(2,1)S(1)} all-to-all(bf16[64,48,128]{2,1,0:T(8,128)(2,1)S(1)} %pad_maximum_fusion), channel_id=1, replica_groups=mesh['dp'=64,'tensor'=8] {'dp'}, dimensions={0} | all-to-all | bytes 1572864 | tf_op jit(solution)/shard_map/all_to_all | solution.py:24
  44.7 1.5 stack.8
  46.2 10.2 %all-to-all-start.2 = ((bf16[8,512,256]{2,1,0:T(8,128)(2,1)}), bf16[8,512,256]{2,1,0:T(8,128)(2,1)S(1)}, u32[]{:S(2)}, u32[]{:S(2)}) async-start(bf16[8,512,256]{2,1,0:T(8,128)(2,1)} %stack.8), calls=%async_computation.3 | async-start | bytes 4194304 | tf_op jit(solution)/shard_map/all_to_all | solution.py:14
  57.1 0.9 fusion.4
  58.6 2.1 copy.53
  60.7 44.1 %all-to-all-done.2 = bf16[8,512,256]{2,1,0:T(8,128)(2,1)S(1)} async-done(((bf16[8,512,256]{2,1,0:T(8,128)(2,1)}), bf16[8,512,256]{2,1,0:T(8,128)(2,1)S(1)}, u32[]{:S(2)}, u32[]{:S(2)}) %all-to-all-start.2) | async-done | bytes 2097184 | tf_op jit(solution)/shard_map/all_to_all | solution.py:14
  104.7 9.1 %all-to-all-start.1 = ((bf16[64,2,44,128]{3,1,2,0:T(2,128)(2,1)}), bf16[64,2,44,128]{3,1,2,0:T(2,128)(2,1)S(1)}, u32[]{:S(2)}, u32[]{:S(2)}) async-start(bf16[64,2,44,128]{3,1,2,0:T(2,128)(2,1)} %copy.53), calls=%async_computation.1 | async-start | bytes 2883584 | tf_op jit(solution)/shard_map/all_to_all | solution.py:24
  113.8 2.5 %copy.56 = bf16[512,8,256]{2,1,0:T(8,128)(2,1)} copy(bf16[512,8,256]{2,0,1:T(8,128)(2,1)S(1)} %bitcast.64) | data formatting | bytes 4194304 | tf_op jit(solution)/shard_map/reshape | solution.py:14
  116.4 2.9 %reshape_reshape.3 = bf16[2,256,2048]{2,1,0:T(8,128)(2,1)S(1)} reshape(bf16[512,8,256]{2,1,0:T(8,128)(2,1)} %copy.56) | data formatting | bytes 4194304 | tf_op jit(solution)/shard_map/reshape;reshape | solution.py:84
  119.2 1.5 convolution_convert_fusion.1
  121.5 2.6 %copy.60 = bf16[64,2,44,128]{3,1,2,0:T(2,128)(2,1)} copy(bf16[64,2,44,128]{3,0,2,1:T(8,128)(2,1)S(1)} %bitcast.70) | data formatting | bytes 2883584 | tf_op jit(solution)/shard_map/reshape | solution.py:31
  124.1 26.1 %all-to-all-done.1 = bf16[64,2,44,128]{3,1,2,0:T(2,128)(2,1)S(1)} async-done(((bf16[64,2,44,128]{3,1,2,0:T(2,128)(2,1)}), bf16[64,2,44,128]{3,1,2,0:T(2,128)(2,1)S(1)}, u32[]{:S(2)}, u32[]{:S(2)}) %all-to-all-start.1) | async-done | bytes 1441824 | tf_op jit(solution)/shard_map/all_to_all | solution.py:24
  150.2 6.5 %all-to-all-start.3 = ((bf16[64,2,44,128]{3,1,2,0:T(2,128)(2,1)}), bf16[64,2,44,128]{3,1,2,0:T(2,128)(2,1)}, u32[]{:S(2)}, u32[]{:S(2)}) async-start(bf16[64,2,44,128]{3,1,2,0:T(2,128)(2,1)} %copy.60), calls=%async_computation.4 | async-start | bytes 2883584 | tf_op jit(solution)/shard_map/all_to_all | solution.py:24
  156.9 1.3 copy.81
  158.2 2.5 %reshape.116 = bf16[2,176,2048]{2,1,0:T(8,128)(2,1)S(1)} reshape(bf16[2,4,44,16,128]{4,3,2,1,0:T(8,128)(2,1)} %bitcast.71) | data formatting | bytes 2883584 | tf_op jit(solution)/shard_map/reshape | solution.py:40
  160.6 3.0 %convolution_convert_fusion = bf16[2,2048,256]{1,2,0:T(8,128)(2,1)} fusion(bf16[2,176,2048]{2,1,0:T(8,128)(2,1)S(1)} %reshape.116, bf16[22,2,8,256]{3,2,1,0:T(8,128)(2,1)} %bitcast.77), kind=kOutput, calls=%fused_computation | convolution fusion | flops 370147328 | bytes 3719168 | tf_op jit(solution)/shard_map/stf,sfd->std/dot_general | solution.py:89
  163.7 29.3 %all-to-all-done.3 = bf16[64,2,44,128]{3,1,2,0:T(2,128)(2,1)} async-done(((bf16[64,2,44,128]{3,1,2,0:T(2,128)(2,1)}), bf16[64,2,44,128]{3,1,2,0:T(2,128)(2,1)}, u32[]{:S(2)}, u32[]{:S(2)}) %all-to-all-start.3) | async-done | bytes 1441824 | tf_op jit(solution)/shard_map/all_to_all | solution.py:24
  192.9 2.9 %copy.61 = bf16[64,2,44,128]{3,1,0,2:T(2,128)(2,1)S(1)} copy(bf16[64,2,44,128]{3,1,2,0:T(2,128)(2,1)} %all-to-all-done.3) | data formatting | bytes 2883584 | tf_op jit(solution)/shard_map/all_to_all | solution.py:24
  196.7 1.4 copy.62
  198.1 6.4 %all-to-all-start.4 = ((bf16[64,44,128]{2,1,0:T(8,128)(2,1)}), bf16[64,44,128]{2,1,0:T(8,128)(2,1)}, u32[]{:S(2)}, u32[]{:S(2)}) async-start(bf16[64,44,128]{2,1,0:T(8,128)(2,1)} %copy.62), calls=%async_computation.5 | async-start | bytes 1572864 | tf_op jit(solution)/shard_map/all_to_all | solution.py:24
  206.1 21.2 %all-to-all-done.4 = bf16[64,44,128]{2,1,0:T(8,128)(2,1)} async-done(((bf16[64,44,128]{2,1,0:T(8,128)(2,1)}), bf16[64,44,128]{2,1,0:T(8,128)(2,1)}, u32[]{:S(2)}, u32[]{:S(2)}) %all-to-all-start.4) | async-done | bytes 720928 | tf_op jit(solution)/shard_map/all_to_all | solution.py:24
  227.2 1.3 convert_bitcast_fusion
  228.5 1.5 copy.63
  (37 shorter events, 6.6 us)
Async XLA Ops:
  10.4 34.3 %copy-start = (bf16[512,256]{1,0:T(8,128)(2,1)S(1)}, bf16[512,256]{1,0:T(8,128)(2,1)}, u32[]{:S(2)}) copy-start(bf16[512,256]{1,0:T(8,128)(2,1)} %param.7) | copy-start | bytes 786436
  46.2 10.7 %copy-start.3 = (s32[32]{0:T(128)S(1)}, s32[32]{0:T(128)}, u32[]{:S(2)}) copy-start(s32[32]{0:T(128)} %param.11) | copy-start | bytes 388
  46.2 58.6 %all-to-all-start.2 = ((bf16[8,512,256]{2,1,0:T(8,128)(2,1)}), bf16[8,512,256]{2,1,0:T(8,128)(2,1)S(1)}, u32[]{:S(2)}, u32[]{:S(2)}) async-start(bf16[8,512,256]{2,1,0:T(8,128)(2,1)} %stack.8), calls=%async_computation.3 | async-start | bytes 4194304 | tf_op jit(solution)/shard_map/all_to_all | solution.py:14
  57.1 0.9 copy-start.1
  104.7 45.5 %all-to-all-start.1 = ((bf16[64,2,44,128]{3,1,2,0:T(2,128)(2,1)}), bf16[64,2,44,128]{3,1,2,0:T(2,128)(2,1)S(1)}, u32[]{:S(2)}, u32[]{:S(2)}) async-start(bf16[64,2,44,128]{3,1,2,0:T(2,128)(2,1)} %copy.53), calls=%async_computation.1 | async-start | bytes 2883584 | tf_op jit(solution)/shard_map/all_to_all | solution.py:24
  150.2 42.8 %all-to-all-start.3 = ((bf16[64,2,44,128]{3,1,2,0:T(2,128)(2,1)}), bf16[64,2,44,128]{3,1,2,0:T(2,128)(2,1)}, u32[]{:S(2)}, u32[]{:S(2)}) async-start(bf16[64,2,44,128]{3,1,2,0:T(2,128)(2,1)} %copy.60), calls=%async_computation.4 | async-start | bytes 2883584 | tf_op jit(solution)/shard_map/all_to_all | solution.py:24
  156.6 73.4 %reduce-scatter.2.cloned.1.call-start = ((), (), s32[]{:S(2)}) async-start(), calls=%async_computation.6 | async-start | bytes 2359296 | tf_op jit(solution)/shard_map/reduce_scatter | solution.py:92
  192.9 3.0 %copy-start.2 = (bf16[128,64]{0,1:T(8,128)(2,1)S(1)}, bf16[128,64]{0,1:T(8,128)(2,1)}, u32[]{:S(2)}) copy-start(bf16[128,64]{0,1:T(8,128)(2,1)} %copy-done.1) | copy-start | bytes 49156
  198.1 29.1 %all-to-all-start.4 = ((bf16[64,44,128]{2,1,0:T(8,128)(2,1)}), bf16[64,44,128]{2,1,0:T(8,128)(2,1)}, u32[]{:S(2)}, u32[]{:S(2)}) async-start(bf16[64,44,128]{2,1,0:T(8,128)(2,1)} %copy.62), calls=%async_computation.5 | async-start | bytes 1572864 | tf_op jit(solution)/shard_map/all_to_all | solution.py:24
Sparse Core Ops, SparseCore 0:
  163.8 37.3 reduce-scatter.1
